TPU v7x, 32 devices: a whole 2x2x4 slice. The times are simulated.
32 devices in a mesh: row: 8 (over y, x, core), col: 4 (over z).
Axes of the slice: x: 2, y: 2, z: 4, core: 2. Of those that a mesh axis runs over, the one named last changes fastest.
Arguments:
- panel_u: bfloat16 [2, 8, 1024, 160], P(None, 'row', 'col'), may hold values from -6 to 6
- panel_v: bfloat16 [2, 8, 1024, 160], P(None, 'row', 'col'), may hold values from -0.0625 to 0.0625
- panel_rank: int32 [2, 8], P(None, 'row'), may hold values from 32 to 160, as said below
- diag_inverse: bfloat16 [1024, 1024], P('col'), as said below
- tile_u: bfloat16 [2, 8, 4, 1024, 160], P(None, 'row', 'col'), may hold values from -6 to 6
- tile_v: bfloat16 [2, 8, 4, 1024, 160], P(None, 'row', 'col'), may hold values from -0.5 to 0.5
- tile_rank: int32 [2, 8, 4], P(None, 'row', 'col'), may hold values from 32 to 160, as said below
- sketch: bfloat16 [2, 8, 4, 1024, 160], P(None, 'row', 'col'), may hold values from -6 to 6
Outputs:
- new_u: float32 [2, 8, 4, 1024, 160], P(None, 'row', 'col')
- new_v: float32 [2, 8, 4, 1024, 160], P(None, 'row', 'col')
Inputs may be any that keep to these rules, and one draw needn't show every extreme that they name: `panel_rank`: some panel tile has rank 160. `tile_rank`: some trailing tile has rank 160. `diag_inverse`: lower triangular with diagonal entries of 1 to 2.
All inputs are finite; a program needn't handle non-finite values.
Results may differ from a plain program's by a relative error of at most 0.0037.
Values may be sent and summed in bfloat16 or wider, within the bound.
No kernel may reach another device: no remote copies, remote signals or barrier semaphores. Data moves between devices by JAX's collectives and lax.ppermute only.
A program may use at most 64 MiB of HBM per device.

v0:
```python
import math
import jax
import jax.numpy as jnp
from jax import lax
from jax.sharding import PartitionSpec as P


def spread(value, axis, source):
    kept = jnp.where(lax.axis_index(axis) == source, value, 0).astype(value.dtype)
    return lax.psum(kept, axis)


def recompress(old_u, old_v, row_u, row_s, col_u, col_s, omega, rank):
    high = lax.Precision.HIGHEST
    width = old_u.shape[1]
    keep_flag = jnp.arange(width, dtype=jnp.int32) < rank
    keep = keep_flag.astype(jnp.float32)
    keep_half = keep_flag.astype(jnp.bfloat16)
    ou_half = old_u * keep_half
    ov_half = old_v * keep_half
    om_half = omega * keep_half
    coupling = jnp.dot(row_s.T, col_s, preferred_element_type=jnp.float32)
    small_left = jnp.dot(ov_half.T, om_half, preferred_element_type=jnp.float32)
    small_right = jnp.dot(col_u.T, om_half, preferred_element_type=jnp.float32)
    ou = ou_half.astype(jnp.float32)
    ov = ov_half.astype(jnp.float32)
    ru = row_u.astype(jnp.float32)
    cu = col_u.astype(jnp.float32)
    sketched = jnp.dot(ou, small_left, precision=high)
    sketched = sketched - jnp.dot(
        ru, jnp.dot(coupling, small_right, precision=high), precision=high
    )
    gram = jnp.dot(sketched.T, sketched, precision=high) + jnp.diag(1.0 - keep)
    lower = jnp.linalg.cholesky(gram)
    basis = lax.linalg.triangular_solve(
        lower, sketched, left_side=False, lower=True, transpose_a=True
    )
    factor = math.sqrt(old_u.shape[0])
    right = jnp.dot(ov, jnp.dot(ou.T, basis, precision=high), precision=high)
    right = right - jnp.dot(
        cu,
        jnp.dot(coupling.T, jnp.dot(ru.T, basis, precision=high), precision=high),
        precision=high,
    )
    return (basis * factor, right / factor)


def on_device(panel_u, panel_v, panel_rank, diag_inverse, tile_u, tile_v, tile_rank, sketch):
    width = panel_u.shape[3]
    keep = (
        jnp.arange(width, dtype=jnp.int32)[None, None, None, :] < panel_rank[:, :, None, None]
    ).astype(jnp.bfloat16)
    full_u, full_v = (
        lax.all_gather(panel_u * keep, "col", axis=2, tiled=True),
        lax.all_gather(panel_v * keep, "col", axis=2, tiled=True),
    )
    inverse = lax.all_gather(diag_inverse, "col", axis=0, tiled=True)
    solved = jnp.einsum(
        "ab,tsbr->tsar", inverse, full_v, preferred_element_type=jnp.float32
    ).astype(jnp.bfloat16)
    col_count = lax.axis_size("col")
    col_place = lax.axis_index("col")
    results_u = []
    results_v = []
    for column in range(tile_u.shape[0]):
        source = column * col_count + col_place
        col_u, col_s = (spread(full_u[0, 0], "row", source), spread(solved[0, 0], "row", source))
        fresh_u, fresh_v = recompress(
            tile_u[column, 0, 0],
            tile_v[column, 0, 0],
            full_u[1, 0],
            solved[1, 0],
            col_u,
            col_s,
            sketch[column, 0, 0],
            tile_rank[column, 0, 0],
        )
        results_u.append(fresh_u)
        results_v.append(fresh_v)
    stacked_u = jnp.stack(results_u)[:, None, None]
    stacked_v = jnp.stack(results_v)[:, None, None]
    return (stacked_u, stacked_v)


def solution(mesh):
    placed = (
        P(None, "row", "col", None),
        P(None, "row", "col", None),
        P(None, "row"),
        P("col", None),
        P(None, "row", "col", None, None),
        P(None, "row", "col", None, None),
        P(None, "row", "col"),
        P(None, "row", "col", None, None),
    )
    return jax.shard_map(
        on_device,
        mesh=mesh,
        in_specs=placed,
        out_specs=(P(None, "row", "col", None, None), P(None, "row", "col", None, None)),
        check_vma=False,
    )
```

profile of v0, /device:TPU:0, one launch (start us, length us, event | category | flops | bytes accessed | tf_op | source)
XLA Modules:
  0.0 269.2 jit_solution(11368111475773620207)
XLA Ops:
  7.2 0.7 all-gather.2.cloned.1.call-update
  8.0 1.3 fusion.77
  9.3 0.6 fusion.71
  10.6 0.7 convert_subtract_fusion
  11.3 0.7 compare_convert_fusion
  12.0 1.1 bitcast_multiply_fusion.15
  13.1 1.4 fusion.24
  14.9 27.4 %all_gather.9 = bf16[2,1,1024,160]{2,3,0,1:T(8,128)(2,1)S(1)} all-gather(bf16[2,1,256,160]{2,3,0,1:T(8,128)(2,1)S(1)} %get-tuple-element.50), channel_id=1, replica_groups=mesh['row'=8,'col'=4] {'col'}, dimensions={2}, use_global_device_ids=true | all-gather | bytes 819200 | tf_op jit(solution)/shard_map/all_gather | solution.py:54
  42.3 26.6 %all_gather.10 = bf16[2,1,1024,160]{2,3,0,1:T(8,128)(2,1)S(1)} all-gather(bf16[2,1,256,160]{2,3,0,1:T(8,128)(2,1)S(1)} %get-tuple-element.51), channel_id=1, replica_groups=mesh['row'=8,'col'=4] {'col'}, dimensions={2}, use_global_device_ids=true | all-gather | bytes 819200 | tf_op jit(solution)/shard_map/all_gather | solution.py:55
  68.9 0.9 select_bitcast_fusion.2
  69.8 6.8 %all-gather.2.cloned.1.call-done = bf16[1024,1024]{1,0:T(8,128)(2,1)} async-done(((bf16[256,1024]{1,0:T(8,128)(2,1)}), bf16[1024,1024]{1,0:T(8,128)(2,1)}) %all-gather.2.cloned.1.call-update) | async-done | bytes 2097168 | tf_op jit(solution)/shard_map/all_gather | solution.py:57
  76.6 2.5 fusion.5
  79.1 0.9 select_bitcast_fusion.3
  81.2 1.5 fusion.45
  82.7 55.3 %all-reduce.6.cloned.1.call-done = (bf16[1024,160]{0,1:T(8,128)(2,1)}, bf16[1024,160]{0,1:T(8,128)(2,1)}, bf16[1024,160]{0,1:T(8,128)(2,1)}, bf16[1024,160]{0,1:T(8,128)(2,1)}) async-done(((bf16[1024,160]{0,1:T(8,128)(2,1)}, bf16[1024,160]{0,1:T(8,128)(2,1)}, bf16[1024,160]{0,1:T(8,128)(2,1)}, bf16[1024,160]{0,1:T(8,128)(2,1)}), (bf16[1024,160]{0,1:T(8,128)(2,1)}, bf16[1024,160]{0,1:T(8,128)(2,1)}, ...) | async-done | bytes 1310736 | tf_op jit(solution)/shard_map/psum | solution.py:10
  138.0 1.4 fusion.23
  139.4 1.2 fusion.35
  141.4 0.7 convolution_add_fusion
  142.3 11.7 %cholesky.174 = f32[128,128]{1,0:T(8,128)S(1)} custom-call(f32[128,128]{1,0:T(8,128)S(1)} %cholesky.211), custom_call_target="Cholesky" | custom-call | tf_op jit(solution)/shard_map/jit(cholesky)/cholesky | solution.py:34
  154.0 0.7 select_reduce_fusion
  154.7 1.4 fusion.27
  156.1 1.2 fusion.36
  158.1 0.7 convolution_add_fusion.1
  159.0 11.9 %cholesky.136 = f32[128,128]{1,0:T(8,128)S(1)} custom-call(f32[128,128]{1,0:T(8,128)S(1)} %cholesky.208), custom_call_target="Cholesky" | custom-call | tf_op jit(solution)/shard_map/jit(cholesky)/cholesky | solution.py:34
  170.9 10.6 %custom-call.15 = f32[1,128,128]{1,2,0:T(8,128)S(1)} custom-call(f32[1,128,128]{2,1,0:T(8,128)} %get-tuple-element.45), custom_call_target="InvertDiagBlocksLowerTriangular" | custom-call | tf_op jit(solution)/shard_map/jit(cholesky)/cholesky | solution.py:34
  181.9 2.9 %cholesky.194 = f32[32,32]{1,0:T(8,128)S(1)} custom-call(f32[32,32]{1,0:T(8,128)S(1)} %convolution_subtract_fusion.6), custom_call_target="Cholesky" | custom-call | tf_op jit(solution)/shard_map/jit(cholesky)/cholesky | solution.py:34
  184.8 0.6 compare_reduce_fusion
  185.5 0.6 compare_reduce_fusion.1
  187.4 0.6 copy-done.6
  188.1 9.8 %custom-call.13 = f32[1,128,128]{1,2,0:T(8,128)S(1)} custom-call(f32[1,128,128]{2,1,0:T(8,128)S(1)} %get-tuple-element.43), custom_call_target="InvertDiagBlocksLowerTriangular" | custom-call | tf_op jit(solution)/shard_map/jit(cholesky)/cholesky | solution.py:34
  198.2 2.9 %cholesky.156 = f32[32,32]{1,0:T(8,128)S(1)} custom-call(f32[32,32]{1,0:T(8,128)S(1)} %convolution_subtract_fusion.7), custom_call_target="Cholesky" | custom-call | tf_op jit(solution)/shard_map/jit(cholesky)/cholesky | solution.py:34
  201.8 0.6 compare_reduce_fusion.3
  203.6 0.7 select_select_fusion.1
  204.3 0.7 slice.139
  205.0 0.8 slice_bitcast_fusion.13
  206.0 0.7 pad_maximum_fusion.6
  206.6 19.7 %custom-call.14 = f32[2,128,128]{1,2,0:T(8,128)S(1)} custom-call(f32[2,128,128]{2,1,0:T(8,128)S(1)} %get-tuple-element.58), custom_call_target="InvertDiagBlocksLowerTriangular" | custom-call | tf_op jit(solution)/shard_map/triangular_solve/custom-call.0 | solution.py:35
  226.3 0.6 copy-done.10
  227.6 1.2 convolution_subtract_fusion.5
  228.8 1.0 fusion.68
  230.3 1.2 fusion.20
  231.5 20.5 %custom-call.16 = f32[2,128,128]{1,2,0:T(8,128)S(1)} custom-call(f32[2,128,128]{2,1,0:T(8,128)} %get-tuple-element.59), custom_call_target="InvertDiagBlocksLowerTriangular" | custom-call | tf_op jit(solution)/shard_map/triangular_solve/custom-call.0 | solution.py:35
  252.0 0.6 copy-done.11
  252.6 0.6 fusion.13
  253.3 1.1 convolution_subtract_fusion.4
  254.4 1.0 fusion.65
  260.1 1.1 maximum_bitcast_fusion.1
  261.2 1.2 maximum_bitcast_fusion
  (68 shorter events, 11.1 us)
Async XLA Ops:
  7.2 7.3 %copy-start.12 = (bf16[2,1,1,1024,160]{3,4,2,1,0:T(8,128)(2,1)S(1)}, bf16[2,1,1,1024,160]{3,4,2,1,0:T(8,128)(2,1)}, u32[]{:S(2)}) copy-start(bf16[2,1,1,1024,160]{3,4,2,1,0:T(8,128)(2,1)} %param.18) | copy-start | bytes 1966084
  7.2 7.3 %copy-start.4 = (bf16[2,1,1,1024,160]{3,4,2,1,0:T(8,128)(2,1)S(1)}, bf16[2,1,1,1024,160]{3,4,2,1,0:T(8,128)(2,1)}, u32[]{:S(2)}) copy-start(bf16[2,1,1,1024,160]{3,4,2,1,0:T(8,128)(2,1)} %param.16) | copy-start | bytes 1966084
  7.2 69.5 %all-gather.2.cloned.1.call-start = ((), (), s32[]{:S(2)}) async-start(), calls=%async_computation | async-start | bytes 2621440 | tf_op jit(solution)/shard_map/all_gather | solution.py:57
  7.9 130.1 %all-reduce.6.cloned.1.call-start = ((), (), s32[]{:S(2)}) async-start(), calls=%async_computation.1 | async-start | bytes 2621440 | tf_op jit(solution)/shard_map/psum | solution.py:10
  79.1 60.3 %copy-start = (bf16[2,1,1024,160]{2,3,0,1:T(8,128)(2,1)}, bf16[2,1,1024,160]{2,3,0,1:T(8,128)(2,1)S(1)}, u32[]{:S(2)}) copy-start(bf16[2,1,1024,160]{2,3,0,1:T(8,128)(2,1)S(1)} %fusion.5) | copy-start | bytes 1966084
  79.1 1.6 copy-start.2
  142.1 14.0 %copy-start.1 = (bf16[2,1,1024,160]{2,3,0,1:T(8,128)(2,1)S(1)}, bf16[2,1,1024,160]{2,3,0,1:T(8,128)(2,1)}, u32[]{:S(2)}) copy-start(bf16[2,1,1024,160]{2,3,0,1:T(8,128)(2,1)} %copy-done) | copy-start | bytes 1966084
  187.4 0.7 copy-start.6
  226.3 0.7 copy-start.10
  227.6 2.7 %copy-start.3 = (bf16[2,1,1,1024,160]{3,4,2,1,0:T(8,128)(2,1)S(1)}, bf16[2,1,1,1024,160]{3,4,2,1,0:T(8,128)(2,1)}, u32[]{:S(2)}) copy-start(bf16[2,1,1,1024,160]{3,4,2,1,0:T(8,128)(2,1)} %param.15) | copy-start | bytes 1966084
  252.0 0.7 copy-start.11
  256.4 1.1 copy-start.5
  256.4 1.1 copy-start.9
  257.5 1.6 copy-start.8
  258.6 1.0 copy-start.7
Sparse Core Ops, SparseCore 0:
  9.6 67.0 all-gather.1
  80.6 57.3 all-reduce.5
where the time goes:
time: 270 us; the launch traced here: 269 us
  other arithmetic  103 us (38%)
  waiting for transfers between devices  62.8 us (23%)
  blocking collectives  54 us (20%)
  matrix products  26.2 us (10%)
  between operations  17.2 us (6%)
  local copies, waits for them, and re-layouts  5.59 us (2%)
    psum x1, waiting for transfers between devices, spread(): return lax.psum(kept, axis)  55.3 us
    another operation x14, other arithmetic, recompress(): lower = jnp.linalg.cholesky(gram)  53.1 us
    another operation x8, other arithmetic, recompress(): lax.linalg.triangular_solve(lower, sketched, left_side=False, lower=True,...  41.6 us
    all_gather x1, blocking collectives, on_device(): lax.all_gather(panel_u * keep, 'col', axis=2, tiled=True)  27.4 us
    all_gather x1, blocking collectives, on_device(): lax.all_gather(panel_v * keep, 'col', axis=2, tiled=True)  26.6 us
    all_gather x1, waiting for transfers between devices, on_device(): inverse = lax.all_gather(diag_inverse, 'col', axis=0, tiled=True)  6.83 us
    another operation x6, matrix products, recompress(): lax.linalg.triangular_solve(lower, sketched, left_side=False, lower=True,...  5.61 us
  transfers between devices with their start and end apart: 2, of which 2 were waited for; matrix products, arithmetic and copies ran while one was open for 4% of the time, Pallas kernels for 0%

commit v1 on v0

--- a/solution.py
+++ b/solution.py
@@ -50,8 +50,17 @@
     keep = (
         jnp.arange(width, dtype=jnp.int32)[None, None, None, :] < panel_rank[:, :, None, None]
     ).astype(jnp.bfloat16)
+    create_copies = lambda shard_in: jnp.concatenate(
+        jax.lax.all_to_all(
+            jnp.stack([shard_in for _ in range(jax.lax.axis_size("col"))], axis=0),
+            axis_name="col",
+            split_axis=0,
+            concat_axis=0,
+        ),
+        axis=2,
+    )
     full_u, full_v = (
-        lax.all_gather(panel_u * keep, "col", axis=2, tiled=True),
+        create_copies(panel_u * keep),
         lax.all_gather(panel_v * keep, "col", axis=2, tiled=True),
     )
     inverse = lax.all_gather(diag_inverse, "col", axis=0, tiled=True)

time: 270 us -> 265 us (0.981)
  starting transfers between devices: 0.08 us -> 6.39 us
  matrix products: 26.2 us -> 20.8 us
  blocking collectives: 54 us -> 49.3 us
    all_gather x1 -> x0, blocking collectives: 27.4 us -> none  [on_device(): lax.all_gather(panel_u * keep, 'col', axis=2, tiled=True)]
    all_gather x1, blocking collectives: 26.6 us -> 49.3 us  [on_device(): lax.all_gather(panel_v * keep, 'col', axis=2, tiled=True)]
    all_to_all x0 -> x1, starting transfers between devices: none -> 6.35 us  [on_device(): jax.lax.all_to_all(jnp.stack([shard_in for _ in range(jax.lax.axis_size('...]
    another operation x6, matrix products: 5.61 us -> 2.68 us  [recompress(): lax.linalg.triangular_solve(lower, sketched, left_side=False, lower=True,...]
  transfers between devices with their start and end apart: 2 -> 3, of which waited for: 2 -> 2; matrix products, arithmetic and copies ran while one was open for 4% -> 4% of each run, Pallas kernels for 0% -> 0%
where the time goes in v1:
time: 265 us
  other arithmetic  102 us (38%)
  waiting for transfers between devices  63.7 us (24%)
  blocking collectives  49.3 us (19%)
  matrix products  20.8 us (8%)
  between operations  17.2 us (6%)
  starting transfers between devices  6.39 us (2%)
  local copies, waits for them, and re-layouts  5.57 us (2%)
    psum x1, waiting for transfers between devices, spread(): return lax.psum(kept, axis)  55.7 us
    another operation x14, other arithmetic, recompress(): lower = jnp.linalg.cholesky(gram)  53.2 us
    all_gather x1, blocking collectives, on_device(): lax.all_gather(panel_v * keep, 'col', axis=2, tiled=True)  49.3 us
    another operation x8, other arithmetic, recompress(): lax.linalg.triangular_solve(lower, sketched, left_side=False, lower=True,...  41 us
    all_gather x1, waiting for transfers between devices, on_device(): inverse = lax.all_gather(diag_inverse, 'col', axis=0, tiled=True)  7.27 us
    all_to_all x1, starting transfers between devices, on_device(): jax.lax.all_to_all(jnp.stack([shard_in for _ in range(jax.lax.axis_size('...  6.35 us
  transfers between devices with their start and end apart: 3, of which 2 were waited for; matrix products, arithmetic and copies ran while one was open for 4% of the time, Pallas kernels for 0%

profile of v1, /device:TPU:0, one launch (start us, length us, event | category | flops | bytes accessed | tf_op | source)
XLA Modules:
  0.0 264.8 jit_solution(15636465008803923956)
XLA Ops:
  7.2 0.7 all-gather.2.cloned.1.call-update
  7.9 0.7 compare_convert_fusion
  8.6 1.2 bitcast_multiply_fusion.14
  9.8 0.9 stack.25
  10.7 6.3 %all-to-all-start = ((bf16[4,2,1,256,160]{3,4,2,1,0:T(8,128)(2,1)}), bf16[4,2,1,256,160]{3,4,2,1,0:T(8,128)(2,1)S(1)}, u32[]{:S(2)}, u32[]{:S(2)}) async-start(bf16[4,2,1,256,160]{3,4,2,1,0:T(8,128)(2,1)} %stack.25), calls=%async_computation | async-start | bytes 1310720 | tf_op jit(solution)/shard_map/all_to_all | solution.py:54
  17.1 0.6 fusion.78
  17.7 0.6 fusion.72
  18.3 0.6 fusion.73
  18.9 0.7 convert_subtract_fusion
  20.3 49.3 %all_gather.6 = bf16[2,1,1024,160]{2,3,0,1:T(8,128)(2,1)S(1)} all-gather(bf16[2,1,256,160]{2,3,0,1:T(8,128)(2,1)S(1)} %get-tuple-element.55), channel_id=1, replica_groups=mesh['row'=8,'col'=4] {'col'}, dimensions={2}, use_global_device_ids=true | all-gather | bytes 819200 | tf_op jit(solution)/shard_map/all_gather | solution.py:64
  69.9 0.8 copy.41
  70.9 0.8 copy.42
  71.7 7.3 %all-gather.2.cloned.1.call-done = bf16[1024,1024]{1,0:T(8,128)(2,1)} async-done(((bf16[256,1024]{1,0:T(8,128)(2,1)}), bf16[1024,1024]{1,0:T(8,128)(2,1)}) %all-gather.2.cloned.1.call-update) | async-done | bytes 2097168 | tf_op jit(solution)/shard_map/all_gather | solution.py:66
  79.0 2.5 fusion.5
  81.4 0.9 select_bitcast_fusion.1
  82.3 0.6 convert_subtract_fusion.1
  82.9 0.5 fusion.46
  83.5 0.5 fusion.45
  84.3 55.7 %all-reduce.6.cloned.1.call-done = (bf16[1024,160]{0,1:T(8,128)(2,1)}, bf16[1024,160]{0,1:T(8,128)(2,1)}, bf16[1024,160]{0,1:T(8,128)(2,1)}, bf16[1024,160]{0,1:T(8,128)(2,1)}) async-done(((bf16[1024,160]{0,1:T(8,128)(2,1)}, bf16[1024,160]{0,1:T(8,128)(2,1)}, bf16[1024,160]{0,1:T(8,128)(2,1)}, bf16[1024,160]{0,1:T(8,128)(2,1)}), (bf16[1024,160]{0,1:T(8,128)(2,1)}, bf16[1024,160]{0,1:T(8,128)(2,1)}, ...) | async-done | bytes 1310736 | tf_op jit(solution)/shard_map/psum | solution.py:10
  140.0 1.3 fusion.23
  141.3 1.2 fusion.35
  143.4 0.7 convolution_add_fusion
  144.3 11.7 %cholesky.174 = f32[128,128]{1,0:T(8,128)S(1)} custom-call(f32[128,128]{1,0:T(8,128)S(1)} %cholesky.211), custom_call_target="Cholesky" | custom-call | tf_op jit(solution)/shard_map/jit(cholesky)/cholesky | solution.py:34
  156.0 0.6 select_reduce_fusion
  156.6 1.3 fusion.27
  158.2 0.7 copy-done.2
  159.7 0.7 convolution_add_fusion.1
  160.5 11.9 %cholesky.136 = f32[128,128]{1,0:T(8,128)S(1)} custom-call(f32[128,128]{1,0:T(8,128)S(1)} %cholesky.208), custom_call_target="Cholesky" | custom-call | tf_op jit(solution)/shard_map/jit(cholesky)/cholesky | solution.py:34
  172.5 10.6 %custom-call.15 = f32[1,128,128]{1,2,0:T(8,128)S(1)} custom-call(f32[1,128,128]{2,1,0:T(8,128)} %get-tuple-element.50), custom_call_target="InvertDiagBlocksLowerTriangular" | custom-call | tf_op jit(solution)/shard_map/jit(cholesky)/cholesky | solution.py:34
  183.1 0.9 constant_dynamic-update-slice_fusion.1
  184.0 0.9 convolution_subtract_fusion.6
  184.9 2.9 %cholesky.194 = f32[32,32]{1,0:T(8,128)S(1)} custom-call(f32[32,32]{1,0:T(8,128)S(1)} %convolution_subtract_fusion.6), custom_call_target="Cholesky" | custom-call | tf_op jit(solution)/shard_map/jit(cholesky)/cholesky | solution.py:34
  187.8 0.6 compare_reduce_fusion
  188.5 0.6 compare_reduce_fusion.1
  190.4 9.8 %custom-call.13 = f32[1,128,128]{1,2,0:T(8,128)S(1)} custom-call(f32[1,128,128]{2,1,0:T(8,128)S(1)} %get-tuple-element.48), custom_call_target="InvertDiagBlocksLowerTriangular" | custom-call | tf_op jit(solution)/shard_map/jit(cholesky)/cholesky | solution.py:34
  200.5 2.9 %cholesky.156 = f32[32,32]{1,0:T(8,128)S(1)} custom-call(f32[32,32]{1,0:T(8,128)S(1)} %convolution_subtract_fusion.7), custom_call_target="Cholesky" | custom-call | tf_op jit(solution)/shard_map/jit(cholesky)/cholesky | solution.py:34
  203.5 0.6 compare_reduce_fusion.2
  204.1 0.6 compare_reduce_fusion.3
  206.1 0.7 pad_maximum_fusion.6
  206.8 19.7 %custom-call.14 = f32[2,128,128]{1,2,0:T(8,128)S(1)} custom-call(f32[2,128,128]{2,1,0:T(8,128)S(1)} %get-tuple-element.63), custom_call_target="InvertDiagBlocksLowerTriangular" | custom-call | tf_op jit(solution)/shard_map/triangular_solve/custom-call.0 | solution.py:35
  226.4 0.6 fusion.15
  228.8 20.5 %custom-call.16 = f32[2,128,128]{1,2,0:T(8,128)S(1)} custom-call(f32[2,128,128]{2,1,0:T(8,128)} %get-tuple-element.64), custom_call_target="InvertDiagBlocksLowerTriangular" | custom-call | tf_op jit(solution)/shard_map/triangular_solve/custom-call.0 | solution.py:35
  249.3 0.6 fusion.13
  251.8 0.8 copy-done.3
  253.1 0.5 fusion.22
  254.1 0.5 fusion.21
  255.7 1.1 maximum_bitcast_fusion.1
  256.8 1.1 maximum_bitcast_fusion
  (82 shorter events, 9.8 us)
Async XLA Ops:
  7.2 71.8 %all-gather.2.cloned.1.call-start = ((), (), s32[]{:S(2)}) async-start(), calls=%async_computation.1 | async-start | bytes 2621440 | tf_op jit(solution)/shard_map/all_gather | solution.py:66
  8.6 8.5 %copy-start.13 = (s32[2,1,1]{0,2,1:T(1,128)S(1)}, s32[2,1,1]{0,2,1:T(1,128)}, u32[]{:S(2)}) copy-start(s32[2,1,1]{0,2,1:T(1,128)} %param.17) | copy-start | bytes 28
  8.6 11.0 %copy-start.6 = (bf16[2,1,1,1024,160]{3,4,2,1,0:T(8,128)(2,1)S(1)}, bf16[2,1,1,1024,160]{3,4,2,1,0:T(8,128)(2,1)}, u32[]{:S(2)}) copy-start(bf16[2,1,1,1024,160]{3,4,2,1,0:T(8,128)(2,1)} %param.16) | copy-start | bytes 1966084
  8.6 11.0 %copy-start.14 = (bf16[2,1,1,1024,160]{3,4,2,1,0:T(8,128)(2,1)S(1)}, bf16[2,1,1,1024,160]{3,4,2,1,0:T(8,128)(2,1)}, u32[]{:S(2)}) copy-start(bf16[2,1,1,1024,160]{3,4,2,1,0:T(8,128)(2,1)} %param.18) | copy-start | bytes 1966084
  10.7 58.8 %all-to-all-start = ((bf16[4,2,1,256,160]{3,4,2,1,0:T(8,128)(2,1)}), bf16[4,2,1,256,160]{3,4,2,1,0:T(8,128)(2,1)S(1)}, u32[]{:S(2)}, u32[]{:S(2)}) async-start(bf16[4,2,1,256,160]{3,4,2,1,0:T(8,128)(2,1)} %stack.25), calls=%async_computation | async-start | bytes 1310720 | tf_op jit(solution)/shard_map/all_to_all | solution.py:54
  17.1 122.9 %all-reduce.6.cloned.1.call-start = ((), (), s32[]{:S(2)}) async-start(), calls=%async_computation.2 | async-start | bytes 2621440 | tf_op jit(solution)/shard_map/psum | solution.py:10
  81.4 1.5 copy-start.4
  84.0 56.0 %copy-start.15 = (bf16[2,1,1,1024,160]{3,4,2,1,0:T(8,128)(2,1)S(1)}, bf16[2,1,1,1024,160]{3,4,2,1,0:T(8,128)(2,1)}, u32[]{:S(2)}) copy-start(bf16[2,1,1,1024,160]{3,4,2,1,0:T(8,128)(2,1)} %param.18) | copy-start | bytes 1966084
  142.6 1.5 copy-start
  143.4 13.3 %copy-start.10 = (bf16[1024,160]{0,1:T(8,128)(2,1)S(1)}, bf16[1024,160]{0,1:T(8,128)(2,1)}, u32[]{:S(2)}) copy-start(bf16[1024,160]{0,1:T(8,128)(2,1)} %get-tuple-element.39) | copy-start | bytes 983044
  144.2 13.8 %copy-start.12 = (bf16[1024,160]{0,1:T(8,128)(2,1)S(1)}, bf16[1024,160]{0,1:T(8,128)(2,1)}, u32[]{:S(2)}) copy-start(bf16[1024,160]{0,1:T(8,128)(2,1)} %get-tuple-element.38) | copy-start | bytes 983044
  144.2 15.0 %copy-start.8 = (f32[160,160]{1,0:T(8,128)}, f32[160,160]{1,0:T(8,128)S(1)}, u32[]{:S(2)}) copy-start(f32[160,160]{1,0:T(8,128)S(1)} %fusion.47) | copy-start | bytes 307204
  158.2 0.7 copy-start.2
  227.1 1.2 copy-start.5
  251.6 0.9 copy-start.3
  251.7 1.4 copy-start.7
  251.7 1.9 copy-start.1
  253.1 1.6 copy-start.11
  254.1 1.0 copy-start.9
Sparse Core Ops, SparseCore 0:
  9.5 69.3 all-gather.1
  82.9 57.0 all-reduce.5
